TPU v7x, 32 devices: a whole 2x2x4 slice. The times are simulated.
32 devices in a mesh: dp: 8 (over y, x, core), fsdp: 4 (over z).
Axes of the slice: x: 2, y: 2, z: 4, core: 2. Of those that a mesh axis runs over, the one named last changes fastest.
Arguments:
- tokens: bfloat16 [64, 1024, 768], P('dp', 'fsdp'), may hold values from -6 to 6
- cotangent: bfloat16 [64, 1024, 768], P('dp', 'fsdp'), may hold values from -6 to 6
- lengths: int32 [8, 8], P('dp'), may hold values from 256 to 1024, as said below
- perm: int32 [8, 8], P('dp'), may hold values from 0 to 7, each once within a row
- ln1_gain: bfloat16 [768], P(('dp', 'fsdp')), may hold values from 0.5 to 1.5
- ln1_bias: bfloat16 [768], P(('dp', 'fsdp')), may hold values from -3 to 3
- w_qkv: bfloat16 [768, 2304], P(('dp', 'fsdp')), may hold values from -0.3125 to 0.3125
- w_out: bfloat16 [768, 768], P(('dp', 'fsdp')), may hold values from -2.5 to 2.5
- ln2_gain: bfloat16 [768], P(('dp', 'fsdp')), may hold values from 0.5 to 1.5
- ln2_bias: bfloat16 [768], P(('dp', 'fsdp')), may hold values from -3 to 3
- w_up: bfloat16 [768, 3072], P(('dp', 'fsdp')), may hold values from -0.21875 to 0.21875
- w_down: bfloat16 [3072, 768], P(('dp', 'fsdp')), may hold values from -0.75 to 0.75
Outputs:
- block_out: bfloat16 [64, 1024, 768], P('dp', 'fsdp')
- d_tokens: bfloat16 [64, 1024, 768], P('dp', 'fsdp')
- grad_ln1_gain: float32 [768], P(('dp', 'fsdp'))
- grad_ln1_bias: float32 [768], P(('dp', 'fsdp'))
- grad_w_qkv: float32 [768, 2304], P(('dp', 'fsdp'))
- grad_w_out: float32 [768, 768], P(('dp', 'fsdp'))
- grad_ln2_gain: float32 [768], P(('dp', 'fsdp'))
- grad_ln2_bias: float32 [768], P(('dp', 'fsdp'))
- grad_w_up: float32 [768, 3072], P(('dp', 'fsdp'))
- grad_w_down: float32 [3072, 768], P(('dp', 'fsdp'))
Inputs may be any that keep to these rules, and one draw needn't show every extreme that they name: lengths[g, p] is the live length of sequence perm[g, p] of dp group g, dealt to fsdp index p // 2 as its micro-batch p % 2; each row holds 1024 and 256 at least once. `perm`: each row is a permutation of the group's 8 sequences.
All inputs are finite; a program needn't handle non-finite values.
Results may differ from a plain program's by a relative error of at most 0.014.
The roundings to bfloat16 on the way count: a program that leaves them out, or rounds other values in their place, can miss the bound.
Values may be sent and summed in bfloat16 or wider, within the bound.
No kernel may reach another device: no remote copies, remote signals or barrier semaphores. Data moves between devices by JAX's collectives and lax.ppermute only.
A program may use at most 384 MiB of HBM per device.

v0:
```python
import math
import jax
import jax.numpy as jnp
from jax import lax
from jax.sharding import PartitionSpec as P

HEADS = 12
DEPTH = 48
epsilon = 1e-05


def gelu_tanh(value):
    inner = 0.7978845608028654 * (value + 0.044715 * value * value * value)
    return 0.5 * value * (1.0 + jnp.tanh(inner))


def norm_parts(seq_rows):
    center = seq_rows - jnp.mean(seq_rows, axis=-1, keepdims=True)
    factor = lax.rsqrt(jnp.mean(center * center, axis=-1, keepdims=True) + epsilon)
    return (center * factor, factor)


def norm_back(grad_normed, normed, factor, gain):
    grad_gain = jnp.sum(grad_normed * normed, axis=0)
    grad_bias = jnp.sum(grad_normed, axis=0)
    scaled = grad_normed * gain
    grad_rows = factor * (
        scaled
        - jnp.mean(scaled, axis=-1, keepdims=True)
        - normed * jnp.mean(scaled * normed, axis=-1, keepdims=True)
    )
    return (grad_rows, grad_gain, grad_bias)


def outer_sum(left, right):
    return lax.dot_general(
        left, right, (((0,), (0,)), ((), ())), preferred_element_type=jnp.float32
    )


def by_transpose(left, right):
    return lax.dot_general(
        left, right, (((1,), (1,)), ((), ())), preferred_element_type=jnp.float32
    )


def split_heads(qkv_low):
    row_count = qkv_low.shape[0]
    model_width = qkv_low.shape[1] // 3
    stacked = qkv_low.reshape(row_count, 3, HEADS, model_width // HEADS)
    return (stacked[:, 0], stacked[:, 1], stacked[:, 2])


def block_mask(first_row, block_rows, key_stop, seq_length):
    query_pos = first_row + lax.iota(jnp.int32, block_rows)
    key_pos = lax.iota(jnp.int32, key_stop)
    return (key_pos[None, :] <= query_pos[:, None]) & (key_pos[None, :] < seq_length)


def attend(qkv_low, seq_length):
    queries, key_rows, values = split_heads(qkv_low)
    row_count, head_count, head_size = queries.shape
    model_width = head_count * head_size
    block_rows = min(512, row_count)
    half_heads = head_count // 2
    factor = 1.0 / math.sqrt(head_size)
    mixed_parts = []
    total_parts = []
    for block_index in range(row_count // block_rows):
        first_row = block_index * block_rows
        key_stop = first_row + block_rows

        def compute(unused, first_row=first_row, key_stop=key_stop):
            allowed = block_mask(first_row, block_rows, key_stop, seq_length)
            query_block = queries[first_row:key_stop]
            outputs = []
            totals = []
            for half_index in range(2):
                low_head = half_index * half_heads
                high_head = low_head + half_heads
                scores = (
                    jnp.einsum(
                        "qhd,khd->hqk",
                        query_block[:, low_head:high_head],
                        key_rows[:key_stop, low_head:high_head],
                        preferred_element_type=jnp.float32,
                    )
                    * factor
                )
                scores = jnp.where(allowed[None], scores, -1e30)
                row_peak = jnp.max(scores, axis=-1, keepdims=True)
                exponent = jnp.exp(scores - row_peak)
                row_total = jnp.sum(exponent, axis=-1, keepdims=True)
                probs_low = (exponent / row_total).astype(jnp.bfloat16)
                outputs.append(
                    jnp.einsum(
                        "hqk,khd->qhd",
                        probs_low,
                        values[:key_stop, low_head:high_head],
                        preferred_element_type=jnp.float32,
                    )
                )
                totals.append((row_peak + jnp.log(row_total))[..., 0])
            return (
                jnp.concatenate(outputs, axis=1).reshape(block_rows, model_width),
                jnp.concatenate(totals, axis=0),
            )

        block_out, block_totals = compute(0)
        mixed_parts.append(block_out)
        total_parts.append(block_totals)
    return (jnp.concatenate(mixed_parts, axis=0), jnp.concatenate(total_parts, axis=1))


def attend_back(qkv_low, log_totals, grad_mixed, seq_length):
    queries, key_rows, values = split_heads(qkv_low)
    row_count, head_count, head_size = queries.shape
    grad_heads = grad_mixed.reshape(row_count, head_count, head_size)
    block_rows = min(512, row_count)
    half_heads = head_count // 2
    factor = 1.0 / math.sqrt(head_size)
    grad_keys = jnp.zeros((row_count, head_count, head_size), jnp.float32)
    grad_values = jnp.zeros((row_count, head_count, head_size), jnp.float32)
    query_parts = []
    for block_index in range(row_count // block_rows):
        first_row = block_index * block_rows
        key_stop = first_row + block_rows

        def compute(unused, first_row=first_row, key_stop=key_stop):
            allowed = block_mask(first_row, block_rows, key_stop, seq_length)
            query_block = queries[first_row:key_stop]
            grad_block = grad_heads[first_row:key_stop]
            query_list = []
            key_list = []
            value_list = []
            for half_index in range(2):
                low_head = half_index * half_heads
                high_head = low_head + half_heads
                scores = (
                    jnp.einsum(
                        "qhd,khd->hqk",
                        query_block[:, low_head:high_head],
                        key_rows[:key_stop, low_head:high_head],
                        preferred_element_type=jnp.float32,
                    )
                    * factor
                )
                scores = jnp.where(allowed[None], scores, -1e30)
                attn_probs = jnp.exp(
                    scores - log_totals[low_head:high_head, first_row:key_stop][..., None]
                )
                grad_probs = jnp.einsum(
                    "qhd,khd->hqk",
                    grad_block[:, low_head:high_head],
                    values[:key_stop, low_head:high_head],
                    preferred_element_type=jnp.float32,
                )
                inner = jnp.sum(attn_probs * grad_probs, axis=-1, keepdims=True)
                grad_scores = (attn_probs * (grad_probs - inner)).astype(jnp.bfloat16)
                query_list.append(
                    jnp.einsum(
                        "hqk,khd->qhd",
                        grad_scores,
                        key_rows[:key_stop, low_head:high_head],
                        preferred_element_type=jnp.float32,
                    )
                    * factor
                )
                key_list.append(
                    jnp.einsum(
                        "hqk,qhd->khd",
                        grad_scores,
                        query_block[:, low_head:high_head],
                        preferred_element_type=jnp.float32,
                    )
                    * factor
                )
                value_list.append(
                    jnp.einsum(
                        "hqk,qhd->khd",
                        attn_probs.astype(jnp.bfloat16),
                        grad_block[:, low_head:high_head],
                        preferred_element_type=jnp.float32,
                    )
                )
            return (
                jnp.concatenate(query_list, axis=1),
                jnp.concatenate(key_list, axis=1),
                jnp.concatenate(value_list, axis=1),
            )

        query_grad, key_grad, value_grad = compute(0)
        query_parts.append(query_grad)
        padding = ((0, row_count - key_stop), (0, 0), (0, 0))
        grad_keys = grad_keys + jnp.pad(key_grad, padding)
        grad_values = grad_values + jnp.pad(value_grad, padding)
    grad_queries = jnp.concatenate(query_parts, axis=0)
    return jnp.concatenate(
        [
            grad_queries.reshape(row_count, -1),
            grad_keys.reshape(row_count, -1),
            grad_values.reshape(row_count, -1),
        ],
        axis=1,
    )


def forward_one(weights, seq_rows, seq_length):
    gain_one, bias_one, qkv_weight, out_weight, gain_two, bias_two, up_weight, down_weight = weights
    branch = 1.0 / math.sqrt(DEPTH)
    live_rows = (lax.iota(jnp.int32, seq_rows.shape[0]) < seq_length)[:, None]
    resid = seq_rows.astype(jnp.float32)
    normed_one, factor_one = norm_parts(resid)
    first_low = (normed_one * gain_one.astype(jnp.float32) + bias_one.astype(jnp.float32)).astype(
        jnp.bfloat16
    )
    qkv_low = jnp.dot(first_low, qkv_weight, preferred_element_type=jnp.float32).astype(
        jnp.bfloat16
    )
    mixed_rows, log_totals = attend(qkv_low, seq_length)
    attn_low = mixed_rows.astype(jnp.bfloat16)
    middle = resid + branch * jnp.dot(attn_low, out_weight, preferred_element_type=jnp.float32)
    normed_two, factor_two = norm_parts(middle)
    second_low = (normed_two * gain_two.astype(jnp.float32) + bias_two.astype(jnp.float32)).astype(
        jnp.bfloat16
    )
    up_proj = jnp.dot(second_low, up_weight, preferred_element_type=jnp.float32)
    gelu_low = gelu_tanh(up_proj).astype(jnp.bfloat16)
    final_rows = middle + branch * jnp.dot(
        gelu_low, down_weight, preferred_element_type=jnp.float32
    )
    block_out = jnp.where(live_rows, final_rows, 0.0).astype(jnp.bfloat16)
    return (block_out, (first_low, qkv_low, log_totals, attn_low, middle, second_low, up_proj))


def backward_one(weights, seq_rows, seq_cotan, seq_length, kept):
    gain_one, bias_one, qkv_weight, out_weight, gain_two, bias_two, up_weight, down_weight = weights
    first_low, qkv_low, log_totals, attn_low, middle, second_low, up_proj = kept
    branch = 1.0 / math.sqrt(DEPTH)
    live_rows = (lax.iota(jnp.int32, seq_rows.shape[0]) < seq_length)[:, None]
    grad_out = jnp.where(live_rows, seq_cotan.astype(jnp.float32), 0.0)
    grad_mlp = (branch * grad_out).astype(jnp.bfloat16)
    gelu_low = gelu_tanh(up_proj).astype(jnp.bfloat16)
    grad_down = outer_sum(gelu_low, grad_mlp)
    grad_gelu = by_transpose(grad_mlp, down_weight)
    unused_value, gelu_pull = jax.vjp(gelu_tanh, up_proj)
    grad_up = gelu_pull(grad_gelu)[0].astype(jnp.bfloat16)
    grad_up_weight = outer_sum(second_low, grad_up)
    grad_second = by_transpose(grad_up, up_weight)
    normed_two, factor_two = norm_parts(middle)
    grad_middle_norm, grad_gain_two, grad_bias_two = norm_back(
        grad_second, normed_two, factor_two, gain_two.astype(jnp.float32)
    )
    grad_middle = grad_out + grad_middle_norm
    grad_attn_out = (branch * grad_middle).astype(jnp.bfloat16)
    grad_out_weight = outer_sum(attn_low, grad_attn_out)
    grad_mixed = by_transpose(grad_attn_out, out_weight).astype(jnp.bfloat16)
    grad_qkv = attend_back(qkv_low, log_totals, grad_mixed, seq_length).astype(jnp.bfloat16)
    grad_qkv_weight = outer_sum(first_low, grad_qkv)
    grad_first = by_transpose(grad_qkv, qkv_weight)
    normed_one, factor_one = norm_parts(seq_rows.astype(jnp.float32))
    grad_input_norm, grad_gain_one, grad_bias_one = norm_back(
        grad_first, normed_one, factor_one, gain_one.astype(jnp.float32)
    )
    grad_rows = (grad_middle + grad_input_norm).astype(jnp.bfloat16)
    return (
        grad_rows,
        (
            grad_gain_one,
            grad_bias_one,
            grad_qkv_weight,
            grad_out_weight,
            grad_gain_two,
            grad_bias_two,
            grad_up_weight,
            grad_down,
        ),
    )


def per_device(
    tokens,
    cotangent,
    lengths,
    perm,
    ln1_gain,
    ln1_bias,
    w_qkv,
    w_out,
    ln2_gain,
    ln2_bias,
    w_up,
    w_down,
):
    group_size = lax.axis_size("fsdp")
    slot_count = tokens.shape[0]
    micro_count = slot_count // group_size
    dealing = perm[0]
    own_lengths = lax.dynamic_slice_in_dim(
        lengths[0], lax.axis_index("fsdp") * micro_count, micro_count
    )
    dealt_rows = jnp.take(tokens, dealing, axis=0)
    dealt_grads = jnp.take(cotangent, dealing, axis=0)
    seq_tokens, seq_cotan = (
        lax.all_to_all(dealt_rows, "fsdp", split_axis=0, concat_axis=1, tiled=True),
        lax.all_to_all(dealt_grads, "fsdp", split_axis=0, concat_axis=1, tiled=True),
    )
    shards = (ln1_gain, ln1_bias, w_qkv, w_out, ln2_gain, ln2_bias, w_up, w_down)
    gathered = (
        lax.all_gather(shards[0], ("dp", "fsdp"), axis=0, tiled=True),
        lax.all_gather(shards[1], ("dp", "fsdp"), axis=0, tiled=True),
        lax.all_gather(shards[2], ("dp", "fsdp"), axis=0, tiled=True),
        lax.all_gather(shards[3], ("dp", "fsdp"), axis=0, tiled=True),
        lax.all_gather(shards[4], ("dp", "fsdp"), axis=0, tiled=True),
        lax.all_gather(shards[5], ("dp", "fsdp"), axis=0, tiled=True),
        lax.all_gather(shards[6], ("dp", "fsdp"), axis=0, tiled=True),
        lax.all_gather(shards[7], ("dp", "fsdp"), axis=0, tiled=True),
    )

    def forward_step(scan_carry, scan_item):
        block_out, kept = forward_one(gathered, scan_item[0], scan_item[1])
        return (scan_carry, (block_out, kept))

    unused_carry, (block_outs, kept_all) = lax.scan(
        forward_step, jnp.int32(0), (seq_tokens, own_lengths)
    )
    back_weights = (
        lax.all_gather(shards[0], ("dp", "fsdp"), axis=0, tiled=True),
        lax.all_gather(shards[1], ("dp", "fsdp"), axis=0, tiled=True),
        lax.all_gather(shards[2], ("dp", "fsdp"), axis=0, tiled=True),
        lax.all_gather(shards[3], ("dp", "fsdp"), axis=0, tiled=True),
        lax.all_gather(shards[4], ("dp", "fsdp"), axis=0, tiled=True),
        lax.all_gather(shards[5], ("dp", "fsdp"), axis=0, tiled=True),
        lax.all_gather(shards[6], ("dp", "fsdp"), axis=0, tiled=True),
        lax.all_gather(shards[7], ("dp", "fsdp"), axis=0, tiled=True),
    )

    def backward_step(totals, scan_item):
        grad_rows, additions = backward_one(
            back_weights, scan_item[0], scan_item[1], scan_item[2], scan_item[3]
        )
        return (tuple((left + right for left, right in zip(totals, additions))), grad_rows)

    zero_grads = tuple((jnp.zeros(piece.shape, jnp.float32) for piece in back_weights))
    totals, grad_tokens = lax.scan(
        backward_step, zero_grads, (seq_tokens, seq_cotan, own_lengths, kept_all), reverse=True
    )
    summed = lax.psum_scatter(totals, ("dp", "fsdp"), scatter_dimension=0, tiled=True)
    returned_out, returned_grad = (
        lax.all_to_all(block_outs, "fsdp", split_axis=1, concat_axis=0, tiled=True),
        lax.all_to_all(grad_tokens, "fsdp", split_axis=1, concat_axis=0, tiled=True),
    )
    inverse = jnp.zeros((slot_count,), jnp.int32).at[dealing].set(lax.iota(jnp.int32, slot_count))
    return (
        jnp.take(returned_out, inverse, axis=0),
        jnp.take(returned_grad, inverse, axis=0),
    ) + tuple(summed)


def solution(mesh):
    placed = (
        P("dp", "fsdp", None),
        P("dp", "fsdp", None),
        P("dp", None),
        P("dp", None),
        P(("dp", "fsdp")),
        P(("dp", "fsdp")),
        P(("dp", "fsdp"), None),
        P(("dp", "fsdp"), None),
        P(("dp", "fsdp")),
        P(("dp", "fsdp")),
        P(("dp", "fsdp"), None),
        P(("dp", "fsdp"), None),
    )
    return jax.shard_map(
        per_device,
        mesh=mesh,
        in_specs=placed,
        out_specs=(
            P("dp", "fsdp", None),
            P("dp", "fsdp", None),
            P(("dp", "fsdp")),
            P(("dp", "fsdp")),
            P(("dp", "fsdp"), None),
            P(("dp", "fsdp"), None),
            P(("dp", "fsdp")),
            P(("dp", "fsdp")),
            P(("dp", "fsdp"), None),
            P(("dp", "fsdp"), None),
        ),
        check_vma=False,
    )
```

profile of v0, /device:TPU:0, one launch (start us, length us, event | category | flops | bytes accessed | tf_op | source)
XLA Modules:
  0.0 1582.8 jit_solution(484979325144604657)
XLA Ops:
  17.0 5.2 broadcast_select_fusion.2
  22.2 6.3 all-to-all-start.2
  29.1 74.7 %all-to-all-done.2 = bf16[8,256,768]{2,1,0:T(8,128)(2,1)S(1)} async-done(((bf16[8,256,768]{2,1,0:T(8,128)(2,1)}), bf16[8,256,768]{2,1,0:T(8,128)(2,1)S(1)}, u32[]{:S(2)}, u32[]{:S(2)}) %all-to-all-start.2) | async-done | bytes 3145760 | tf_op jit(solution)/shard_map/all_to_all | solution.py:306
  103.9 4.8 all-to-all-start
  109.9 96.4 %all-reduce.11 = (bf16[768]{0:T(1024)(128)(2,1)S(1)}, bf16[768]{0:T(1024)(128)(2,1)S(1)}, bf16[768]{0:T(1024)(128)(2,1)S(1)}, bf16[768]{0:T(1024)(128)(2,1)S(1)}) all-reduce(bf16[768]{0:T(1024)(128)(2,1)S(1)} %dynamic-update-slice, bf16[768]{0:T(1024)(128)(2,1)S(1)} %dynamic-update-slice.1, ...), channel_id=1, replica_groups=mesh['dp'=8,'fsdp'=4] {'dp','fsdp'}, use_global_device_ids=true, to_apply=%add.2 | all-reduce | flops 3072 | bytes 12288
  210.9 62.9 %all-gather.9.cloned.1.call-done = bf16[768,3072]{1,0:T(8,128)(2,1)} async-done(((bf16[24,3072]{1,0:T(8,128)(2,1)}), bf16[768,3072]{1,0:T(8,128)(2,1)}) %all-gather.9.cloned.1.call-update) | async-done | bytes 4718608 | tf_op jit(solution)/shard_map/all_gather | solution.py:316
  273.7 64.6 %all-gather.11.cloned.1.call-done = bf16[3072,768]{1,0:T(8,128)(2,1)} async-done(((bf16[96,768]{1,0:T(8,128)(2,1)}), bf16[3072,768]{1,0:T(8,128)(2,1)}) %all-gather.11.cloned.1.call-update) | async-done | bytes 4718608 | tf_op jit(solution)/shard_map/all_gather | solution.py:317
  338.3 221.6 %while.55 = (s32[]{:T(128)}, bf16[2,1024,768]{1,2,0:T(8,128)(2,1)}, bf16[2,1024,768]{1,2,0:T(8,128)(2,1)}, bf16[2,1024,2304]{2,1,0:T(8,128)(2,1)}, f32[2,12,1024...) while((s32[]{:T(128)}, bf16[2,1024,768]{1,2,0:T(8,128)(2,1)}, ...), condition=%wide.region_13.15_spmd, body=%wide.region_0.14_spmd.sunk | while | flops 17094704128 | bytes 421247968 | solution.py:324
  368.3 8.6 bitcast_dynamic-update-slice_fusion.10
  376.9 6.7 copy.143
  396.0 6.2 fusion.362
  402.2 8.7 fusion.363
  411.0 6.5 fusion.366
  436.3 11.4 bitcast_dynamic-update-slice_fusion.11
  447.7 10.3 bitcast_dynamic-update-slice_fusion.12
  468.2 8.7 bitcast_dynamic-update-slice_fusion.10
  476.9 6.7 copy.143
  496.0 6.2 fusion.362
  502.2 8.7 fusion.363
  510.9 6.5 fusion.366
  536.2 11.6 bitcast_dynamic-update-slice_fusion.11
  547.9 10.3 bitcast_dynamic-update-slice_fusion.12
  561.8 450.0 %while.56 = (s32[]{:T(128)}, f32[768]{0:T(1024)}, f32[768]{0:T(1024)}, f32[768,2304]{1,0:T(8,128)}, f32[768,768]{1,0:T(8,128)}, /*index=5*/f32[768]{0:T(1024)}, ...) while((s32[]{:T(128)}, f32[768]{0:T(1024)}, ...), condition=%wide.region_32.34_spmd.clone, body=%wide.region_15.33_spmd.clone.sunk | while | flops 35389038592 | bytes 976789248 | solution.py:345
  584.3 5.5 constant_dynamic-slice_fusion.7
  589.7 6.7 copy.145
  602.1 19.4 %fusion.418 = bf16[1024,3072]{1,0:T(8,128)(2,1)} fusion(f32[2,1024,3072]{2,1,0:T(8,128)} %get-tuple-element.1590, s32[]{:T(128)S(6)} %sub.736, bf16[3072,768]{1,0:T(8,128)(2,1)} %get-tuple-element.1589, pred[1024]{0:T(1024)(128)(4,1)S(1)} %copy-done.73, bf16[2,1024,768]{2,1,0:T(8,128)(2,1)} %get-tuple-element.1587), kind=kOutput, calls=%fused_computation.129.clone.1 | convolution fusion | flops 4910481408 | bytes 25167872 | tf_op jit(solution)/shard_map/while/body/eval_jaxpr/dot_general | solution.py:42
  621.6 10.1 multiply_reduce_fusion.17
  643.6 7.5 select_add_fusion.18
  652.2 5.9 multiply_reduce_fusion.18
  658.1 7.3 multiply_convert_fusion.13
  675.5 13.4 select_add_fusion.19
  696.8 6.4 fusion.427
  703.2 6.4 fusion.429
  711.2 6.4 fusion.436
  717.6 18.3 %multiply_reduce_fusion.19 = (f32[6,512]{1,0:T(8,128)S(1)}, f32[6,512]{1,0:T(8,128)S(1)}, f32[6,512,1024]{2,1,0:T(8,128)}) fusion(f32[6,512,1024]{2,1,0:T(8,128)} %copy-done.12, f32[6,512]{1,0:T(8,128)S(1)} %copy-done.43, pred[512,1024]{1,0:T(8,128)(4,1)S(1)} %copy-done.19, f32[6,512,1024]{2,1,0:T(8,128)} %fusion.436, f32[6,512]{1,0:T(8,128)S(1)} %copy-done.45, ...), kind=kOutput, calls=%fused_computation.148.clone.1 | convolution fusion | flops 434104320 | bytes 52486144 | tf_op jit(solution)/shard_map/while/body/eval_jaxpr/qhd,khd->hqk/dot_general | solution.py:152
  735.8 17.5 %multiply_convert_fusion.14 = (bf16[6,512,1024]{2,1,0:T(8,128)(2,1)S(1)}, bf16[6,512,1024]{2,1,0:T(8,128)(2,1)S(1)}) fusion(f32[6,512,1024]{2,1,0:T(8,128)} %get-tuple-element.1440, f32[6,512,1024]{2,1,0:T(8,128)} %copy-done.12, f32[6,512]{1,0:T(8,128)S(1)} %get-tuple-element.1441, f32[6,512]{1,0:T(8,128)S(1)} %copy-done.43, ...), kind=kLoop, calls=%fused_computation.147.clone.1 | loop fusion | flops 37748736 | bytes 63488000 | tf_op jit(solution)/shard_map/while/body/eval_jaxpr/convert_element_type | solution.py:159
  765.5 7.0 fusion.442
  774.4 7.8 select_add_fusion.15
  799.4 5.5 constant_dynamic-slice_fusion.7
  804.9 6.7 copy.145
  817.3 19.5 %fusion.418 = bf16[1024,3072]{1,0:T(8,128)(2,1)} fusion(f32[2,1024,3072]{2,1,0:T(8,128)} %get-tuple-element.1590, s32[]{:T(128)S(6)} %sub.736, bf16[3072,768]{1,0:T(8,128)(2,1)} %get-tuple-element.1589, pred[1024]{0:T(1024)(128)(4,1)S(1)} %copy-done.73, bf16[2,1024,768]{2,1,0:T(8,128)(2,1)} %get-tuple-element.1587), kind=kOutput, calls=%fused_computation.129.clone.1 | convolution fusion | flops 4910481408 | bytes 25167872 | tf_op jit(solution)/shard_map/while/body/eval_jaxpr/dot_general | solution.py:42
  836.8 10.1 multiply_reduce_fusion.17
  856.0 4.6 select_add_fusion.16
  860.7 9.9 select_add_fusion.18
  871.6 5.9 multiply_reduce_fusion.18
  877.6 7.3 multiply_convert_fusion.13
  894.9 14.8 select_add_fusion.19
  917.6 6.4 fusion.427
  924.0 6.4 fusion.429
  932.0 6.4 fusion.436
  938.4 18.3 %multiply_reduce_fusion.19 = (f32[6,512]{1,0:T(8,128)S(1)}, f32[6,512]{1,0:T(8,128)S(1)}, f32[6,512,1024]{2,1,0:T(8,128)}) fusion(f32[6,512,1024]{2,1,0:T(8,128)} %copy-done.12, f32[6,512]{1,0:T(8,128)S(1)} %copy-done.43, pred[512,1024]{1,0:T(8,128)(4,1)S(1)} %copy-done.19, f32[6,512,1024]{2,1,0:T(8,128)} %fusion.436, f32[6,512]{1,0:T(8,128)S(1)} %copy-done.45, ...), kind=kOutput, calls=%fused_computation.148.clone.1 | convolution fusion | flops 434104320 | bytes 52486144 | tf_op jit(solution)/shard_map/while/body/eval_jaxpr/qhd,khd->hqk/dot_general | solution.py:152
  956.7 17.5 %multiply_convert_fusion.14 = (bf16[6,512,1024]{2,1,0:T(8,128)(2,1)S(1)}, bf16[6,512,1024]{2,1,0:T(8,128)(2,1)S(1)}) fusion(f32[6,512,1024]{2,1,0:T(8,128)} %get-tuple-element.1440, f32[6,512,1024]{2,1,0:T(8,128)} %copy-done.12, f32[6,512]{1,0:T(8,128)S(1)} %get-tuple-element.1441, f32[6,512]{1,0:T(8,128)S(1)} %copy-done.43, ...), kind=kLoop, calls=%fused_computation.147.clone.1 | loop fusion | flops 37748736 | bytes 63488000 | tf_op jit(solution)/shard_map/while/body/eval_jaxpr/convert_element_type | solution.py:159
  986.3 7.0 fusion.442
  995.2 7.8 select_add_fusion.15
  1015.1 4.9 copy.119
  1023.7 8.8 copy.110
  1032.5 68.9 %all-to-all-done.3 = bf16[2,1024,768]{2,0,1:T(2,128)(2,1)S(1)} async-done(((bf16[2,1024,768]{2,0,1:T(2,128)(2,1)}), bf16[2,1024,768]{2,0,1:T(2,128)(2,1)S(1)}, u32[]{:S(2)}, u32[]{:S(2)}) %all-to-all-start.3) | async-done | bytes 3145760 | tf_op jit(solution)/shard_map/all_to_all | solution.py:351
  1101.4 4.7 all-to-all-start.1
  1106.8 93.8 %all-reduce.10 = (f32[768]{0:T(1024)S(1)}, f32[768]{0:T(1024)S(1)}, f32[768]{0:T(1024)S(1)}, f32[768]{0:T(1024)S(1)}) all-reduce(f32[768]{0:T(1024)S(1)} %copy-done.71, f32[768]{0:T(1024)S(1)} %copy-done.68, f32[768]{0:T(1024)S(1)} %copy-done.65, f32[768]{0:T(1024)S(1)} %get-tuple-element.640), channel_id=2, replica_groups=mesh['dp'=8,'fsdp'=4] {'dp','fsdp'}, use_global_device_ids=true, to_apply=%region_33.35.clone | all-reduce | flops 3072 | bytes 24576
  1210.3 4.5 gather_fusion.1
  1214.9 6.3 broadcast_select_fusion
  1221.2 71.3 %reduce-scatter.5.cloned.1.call-done = f32[24,2304]{1,0:T(8,128)} async-done(((f32[768,2304]{1,0:T(8,128)}), f32[24,2304]{1,0:T(8,128)}) %reduce-scatter.5.cloned.1.call-update) | async-done | bytes 221200 | tf_op jit(solution)/shard_map/reduce_scatter | solution.py:348
  1292.4 141.6 %reduce-scatter.9.cloned.1.call-done = f32[24,3072]{1,0:T(8,128)} async-done(((f32[768,3072]{1,0:T(8,128)}), f32[24,3072]{1,0:T(8,128)}) %reduce-scatter.9.cloned.1.call-update) | async-done | bytes 294928 | tf_op jit(solution)/shard_map/reduce_scatter | solution.py:348
  1434.1 141.6 %reduce-scatter.11.cloned.1.call-done = f32[96,768]{1,0:T(8,128)} async-done(((f32[3072,768]{1,0:T(8,128)}), f32[96,768]{1,0:T(8,128)}) %reduce-scatter.11.cloned.1.call-update) | async-done | bytes 294928 | tf_op jit(solution)/shard_map/reduce_scatter | solution.py:348
  (633 shorter events, 251.2 us)
Async XLA Ops:
  7.2 203.7 %all-gather.7.cloned.1.call-start = ((), (), s32[]{:S(2)}) async-start(), calls=%async_computation.9 | async-start | bytes 1216512 | tf_op jit(solution)/shard_map/all_gather | solution.py:313
  7.9 203.0 %all-gather.5.cloned.1.call-start = ((), (), s32[]{:S(2)}) async-start(), calls=%async_computation.8 | async-start | bytes 3649536 | tf_op jit(solution)/shard_map/all_gather | solution.py:312
  8.7 265.1 %all-gather.9.cloned.1.call-start = ((), (), s32[]{:S(2)}) async-start(), calls=%async_computation.10 | async-start | bytes 4866048 | tf_op jit(solution)/shard_map/all_gather | solution.py:316
  22.2 81.7 %all-to-all-start.2 = ((bf16[8,256,768]{2,1,0:T(8,128)(2,1)}), bf16[8,256,768]{2,1,0:T(8,128)(2,1)S(1)}, u32[]{:S(2)}, u32[]{:S(2)}) async-start(bf16[8,256,768]{2,1,0:T(8,128)(2,1)} %get-tuple-element.1064), calls=%async_computation.2 | async-start | bytes 6291456 | tf_op jit(solution)/shard_map/all_to_all | solution.py:306
  28.6 309.8 %all-gather.11.cloned.1.call-start = ((), (), s32[]{:S(2)}) async-start(), calls=%async_computation.11 | async-start | bytes 4866048 | tf_op jit(solution)/shard_map/all_gather | solution.py:317
  103.9 102.4 %copy-start.91 = (s32[1,8]{1,0:T(1,128)S(1)}, s32[1,8]{1,0:T(1,128)}, u32[]{:S(2)}) copy-start(s32[1,8]{1,0:T(1,128)} %param.20) | copy-start | bytes 100
  103.9 104.9 %all-to-all-start = ((bf16[8,256,768]{2,1,0:T(8,128)(2,1)}), bf16[8,256,768]{2,1,0:T(8,128)(2,1)}, u32[]{:S(2)}, u32[]{:S(2)}) async-start(bf16[8,256,768]{2,1,0:T(8,128)(2,1)} %get-tuple-element.1065), calls=%async_computation | async-start | bytes 6291456 | tf_op jit(solution)/shard_map/all_to_all | solution.py:305
  108.7 1112.5 %reduce-scatter.7.cloned.1.call-start = ((), (), s32[]{:S(2)}) async-start(), calls=%async_computation.13 | async-start | bytes 2433024 | tf_op jit(solution)/shard_map/reduce_scatter | solution.py:348
  428.6 7.7 slice-start.4
  436.3 11.4 copy-start.40
  436.3 11.4 copy-start.79
  447.7 12.0 copy-start.8
  447.7 12.0 copy-start.53
  447.7 12.0 copy-start.57
  447.7 12.0 copy-start.75
  447.7 12.0 copy-start.77
  528.5 7.7 slice-start.4
  536.2 11.6 copy-start.40
  536.2 11.6 copy-start.79
  547.8 12.0 copy-start.8
  547.8 12.0 copy-start.53
  547.9 12.0 copy-start.57
  547.9 12.0 copy-start.75
  547.9 12.0 copy-start.77
  570.2 11.1 copy-start.9
  583.8 12.7 copy-start.4
  600.1 72.0 %copy-start.15 = (bf16[1024,12,64]{0,2,1:T(8,128)(2,1)}, bf16[1024,12,64]{0,2,1:T(8,128)(2,1)S(1)}, u32[]{:S(2)}) copy-start(bf16[1024,12,64]{0,2,1:T(8,128)(2,1)S(1)} %get-tuple-element.1428) | copy-start | bytes 4718596 | tf_op jit(solution)/shard_map/while
  621.6 10.1 copy-start.5
  621.6 10.1 copy-start.24
  635.9 7.8 slice-start.8
  643.6 7.5 copy-start.17
  665.5 8.0 slice-start
  761.1 13.3 slice-start.6
  765.5 8.9 slice-start.7
  774.4 7.9 copy-start.36
  774.4 10.8 copy-start.49
  774.4 10.8 copy-start.55
  774.4 10.8 copy-start.59
  774.4 10.8 copy-start.62
  785.4 11.1 copy-start.9
  798.9 12.7 copy-start.4
  815.2 76.3 %copy-start.15 = (bf16[1024,12,64]{0,2,1:T(8,128)(2,1)}, bf16[1024,12,64]{0,2,1:T(8,128)(2,1)S(1)}, u32[]{:S(2)}) copy-start(bf16[1024,12,64]{0,2,1:T(8,128)(2,1)S(1)} %get-tuple-element.1428) | copy-start | bytes 4718596 | tf_op jit(solution)/shard_map/while
  836.8 10.1 copy-start.5
  836.8 10.1 copy-start.24
  851.1 9.6 slice-start.8
  860.7 9.9 copy-start.17
  884.9 8.0 slice-start
  981.9 13.3 slice-start.6
  986.3 8.9 slice-start.7
  995.2 7.9 copy-start.36
  995.2 10.8 copy-start.49
  995.2 10.8 copy-start.55
  995.2 10.8 copy-start.59
  995.2 10.8 copy-start.62
  1011.9 280.6 %reduce-scatter.5.cloned.1.call-start = ((), (), s32[]{:S(2)}) async-start(), calls=%async_computation.12 | async-start | bytes 7299072 | tf_op jit(solution)/shard_map/reduce_scatter | solution.py:348
  1012.4 421.6 %reduce-scatter.9.cloned.1.call-start = ((), (), s32[]{:S(2)}) async-start(), calls=%async_computation.14 | async-start | bytes 9732096 | tf_op jit(solution)/shard_map/reduce_scatter | solution.py:348
  1013.2 562.5 %reduce-scatter.11.cloned.1.call-start = ((), (), s32[]{:S(2)}) async-start(), calls=%async_computation.15 | async-start | bytes 9732096 | tf_op jit(solution)/shard_map/reduce_scatter | solution.py:348
  1020.0 81.4 %all-to-all-start.3 = ((bf16[2,1024,768]{2,0,1:T(2,128)(2,1)}), bf16[2,1024,768]{2,0,1:T(2,128)(2,1)S(1)}, u32[]{:S(2)}, u32[]{:S(2)}) async-start(bf16[2,1024,768]{2,0,1:T(2,128)(2,1)} %copy.119), calls=%async_computation.3 | async-start | bytes 6291456 | tf_op jit(solution)/shard_map/all_to_all | solution.py:351
  1032.5 73.6 %copy-start.93 = (s32[1,8]{1,0:T(1,128)S(1)}, s32[1,8]{1,0:T(1,128)}, u32[]{:S(2)}) copy-start(s32[1,8]{1,0:T(1,128)} %param.21) | copy-start | bytes 100
  1032.5 74.3 %copy-start.65 = (f32[768]{0:T(1024)S(1)}, f32[768]{0:T(1024)}, u32[]{:S(2)}) copy-start(f32[768]{0:T(1024)} %get-tuple-element.639) | copy-start | bytes 9220
  1032.5 74.3 %copy-start.68 = (f32[768]{0:T(1024)S(1)}, f32[768]{0:T(1024)}, u32[]{:S(2)}) copy-start(f32[768]{0:T(1024)} %get-tuple-element.636) | copy-start | bytes 9220
  1032.5 74.3 %copy-start.71 = (f32[768]{0:T(1024)S(1)}, f32[768]{0:T(1024)}, u32[]{:S(2)}) copy-start(f32[768]{0:T(1024)} %get-tuple-element.635) | copy-start | bytes 9220
  1101.4 102.2 %all-to-all-start.1 = ((bf16[2,1024,768]{2,0,1:T(2,128)(2,1)}), bf16[2,1024,768]{2,0,1:T(2,128)(2,1)}, u32[]{:S(2)}, u32[]{:S(2)}) async-start(bf16[2,1024,768]{2,0,1:T(2,128)(2,1)} %copy.110), calls=%async_computation.1 | async-start | bytes 6291456 | tf_op jit(solution)/shard_map/all_to_all | solution.py:350
  1214.9 360.9 %copy-start.1 = (bf16[8,256,768]{2,1,0:T(8,128)(2,1)S(1)}, bf16[8,256,768]{2,1,0:T(8,128)(2,1)}, u32[]{:S(2)}) copy-start(bf16[8,256,768]{2,1,0:T(8,128)(2,1)} %param.19) | copy-start | bytes 9437188
  (141 other events, 491.0 us)
Sparse Core Ops, SparseCore 0:
  10.8 97.0 all-gather.6
  110.7 97.8 all-gather.4
  211.3 62.3 all-gather.8
  276.4 61.8 all-gather.10
  1012.0 153.8 reduce-scatter.6
  1172.0 120.4 reduce-scatter.4
  1298.9 135.1 reduce-scatter.8
  1440.6 135.1 reduce-scatter.10
where the time goes:
time: 1590 us; the launch traced here: 1580 us
  waiting for transfers between devices  630 us (40%)
  matrix products  427 us (27%)
  blocking collectives  190 us (12%)
  local copies, waits for them, and re-layouts  150 us (9%)
  other arithmetic  112 us (7%)
  loops' own time  38.4 us (2%)
  starting transfers between devices  19.8 us (1%)
    reduce_scatter x4, waiting for transfers between devices, per_device(): lax.psum_scatter(totals, ('dp', 'fsdp'), scatter_dimension=0, tiled=True)  355 us
    unnamed x2, blocking collectives  190 us
    dot_general x8, matrix products, by_transpose(): lax.dot_general(left, right, (((1,), (1,)), ((), ())), preferred_element_...  76.1 us
    all_to_all x1, waiting for transfers between devices, per_device(): lax.all_to_all(dealt_grads, 'fsdp', split_axis=0, concat_axis=1, tiled=True)  74.7 us
    all_to_all x1, waiting for transfers between devices, per_device(): lax.all_to_all(grad_tokens, 'fsdp', split_axis=1, concat_axis=0, tiled=True)  68.9 us
    dot_general x8, matrix products, outer_sum(): lax.dot_general(left, right, (((0,), (0,)), ((), ())), preferred_element_...  68.7 us
    all_gather x1, waiting for transfers between devices, per_device(): lax.all_gather(shards[7], ('dp', 'fsdp'), axis=0, tiled=True)  64.6 us
    dot_general x8, matrix products, compute(): jnp.einsum('qhd,khd->hqk', grad_block[:, low_head:high_head], values[:key...  63.3 us
  transfers between devices with their start and end apart: 12, of which 7 were waited for; matrix products, arithmetic and copies ran while one was open for 3% of the time, Pallas kernels for 0%

commit v1 on v0

--- a/solution.py
+++ b/solution.py
@@ -303,7 +303,15 @@
     dealt_grads = jnp.take(cotangent, dealing, axis=0)
     seq_tokens, seq_cotan = (
         lax.all_to_all(dealt_rows, "fsdp", split_axis=0, concat_axis=1, tiled=True),
-        lax.all_to_all(dealt_grads, "fsdp", split_axis=0, concat_axis=1, tiled=True),
+        jnp.concatenate(
+            lax.all_to_all(
+                jnp.stack(jnp.split(dealt_grads, lax.axis_size("fsdp"), axis=0), axis=0),
+                "fsdp",
+                0,
+                0,
+            ),
+            axis=1,
+        ),
     )
     shards = (ln1_gain, ln1_bias, w_qkv, w_out, ln2_gain, ln2_bias, w_up, w_down)
     gathered = (

time: 1590 us -> 1580 us (level)
  waiting for transfers between devices: 630 us -> 611 us
    all_gather x1, waiting for transfers between devices: 62.9 us -> 42.7 us  [per_device(): lax.all_gather(shards[6], ('dp', 'fsdp'), axis=0, tiled=True)]
where the time goes in v1:
time: 1580 us; the launch traced here: 1570 us
  waiting for transfers between devices  611 us (39%)
  matrix products  428 us (27%)
  blocking collectives  200 us (13%)
  local copies, waits for them, and re-layouts  150 us (9%)
  other arithmetic  113 us (7%)
  loops' own time  38.4 us (2%)
  starting transfers between devices  19.8 us (1%)
    reduce_scatter x4, waiting for transfers between devices, per_device(): lax.psum_scatter(totals, ('dp', 'fsdp'), scatter_dimension=0, tiled=True)  355 us
    unnamed x2, blocking collectives  200 us
    dot_general x8, matrix products, by_transpose(): lax.dot_general(left, right, (((1,), (1,)), ((), ())), preferred_element_...  76.1 us
    all_to_all x1, waiting for transfers between devices, per_device(): lax.all_to_all(jnp.stack(jnp.split(dealt_grads, lax.axis_size('fsdp'), ax...  75 us
    all_to_all x1, waiting for transfers between devices, per_device(): lax.all_to_all(grad_tokens, 'fsdp', split_axis=1, concat_axis=0, tiled=True)  68.9 us
    dot_general x8, matrix products, outer_sum(): lax.dot_general(left, right, (((0,), (0,)), ((), ())), preferred_element_...  68.9 us
    all_gather x1, waiting for transfers between devices, per_device(): lax.all_gather(shards[7], ('dp', 'fsdp'), axis=0, tiled=True)  64.6 us
    dot_general x8, matrix products, compute(): jnp.einsum('qhd,khd->hqk', grad_block[:, low_head:high_head], values[:key...  63.3 us
  transfers between devices with their start and end apart: 12, of which 7 were waited for; matrix products, arithmetic and copies ran while one was open for 3% of the time, Pallas kernels for 0%

profile of v1, /device:TPU:0, one launch (start us, length us, event | category | flops | bytes accessed | tf_op | source)
XLA Modules:
  0.0 1574.1 jit_solution(1618832858144463599)
XLA Ops:
  12.5 4.4 gather_fusion
  23.3 6.3 all-to-all-start.2
  30.2 75.0 %all-to-all-done.2 = bf16[4,2,256,768]{3,2,1,0:T(8,128)(2,1)S(1)} async-done(((bf16[4,2,256,768]{3,2,1,0:T(8,128)(2,1)}), bf16[4,2,256,768]{3,2,1,0:T(8,128)(2,1)S(1)}, u32[]{:S(2)}, u32[]{:S(2)}) %all-to-all-start.2) | async-done | bytes 3145760 | tf_op jit(solution)/shard_map/all_to_all | solution.py:307
  105.2 4.8 all-to-all-start
  111.2 106.0 %all-reduce.11 = (bf16[768]{0:T(1024)(128)(2,1)S(1)}, bf16[768]{0:T(1024)(128)(2,1)S(1)}, bf16[768]{0:T(1024)(128)(2,1)S(1)}, bf16[768]{0:T(1024)(128)(2,1)S(1)}) all-reduce(bf16[768]{0:T(1024)(128)(2,1)S(1)} %dynamic-update-slice, bf16[768]{0:T(1024)(128)(2,1)S(1)} %dynamic-update-slice.1, ...), channel_id=1, replica_groups=mesh['dp'=8,'fsdp'=4] {'dp','fsdp'}, use_global_device_ids=true, to_apply=%add.2 | all-reduce | flops 3072 | bytes 12288
  221.8 42.7 %all-gather.9.cloned.1.call-done = bf16[768,3072]{1,0:T(8,128)(2,1)} async-done(((bf16[24,3072]{1,0:T(8,128)(2,1)}), bf16[768,3072]{1,0:T(8,128)(2,1)}) %all-gather.9.cloned.1.call-update) | async-done | bytes 4718608 | tf_op jit(solution)/shard_map/all_gather | solution.py:324
  264.5 64.6 %all-gather.11.cloned.1.call-done = bf16[3072,768]{1,0:T(8,128)(2,1)} async-done(((bf16[96,768]{1,0:T(8,128)(2,1)}), bf16[3072,768]{1,0:T(8,128)(2,1)}) %all-gather.11.cloned.1.call-update) | async-done | bytes 4718608 | tf_op jit(solution)/shard_map/all_gather | solution.py:325
  329.1 221.5 %while.55 = (s32[]{:T(128)}, bf16[2,1024,768]{1,2,0:T(8,128)(2,1)}, bf16[2,1024,768]{1,2,0:T(8,128)(2,1)}, bf16[2,1024,2304]{2,1,0:T(8,128)(2,1)}, f32[2,12,1024...) while((s32[]{:T(128)}, bf16[2,1024,768]{1,2,0:T(8,128)(2,1)}, ...), condition=%wide.region_13.15_spmd, body=%wide.region_0.14_spmd.sunk | while | flops 17094704128 | bytes 421247968 | solution.py:332
  359.1 8.6 bitcast_dynamic-update-slice_fusion.10
  367.7 6.7 copy.143
  386.8 6.2 fusion.362
  392.9 8.7 fusion.363
  401.7 6.5 fusion.366
  427.0 11.4 bitcast_dynamic-update-slice_fusion.11
  438.5 10.3 bitcast_dynamic-update-slice_fusion.12
  459.0 8.7 bitcast_dynamic-update-slice_fusion.10
  467.6 6.7 copy.143
  486.7 6.2 fusion.362
  492.9 8.7 fusion.363
  501.7 6.5 fusion.366
  526.9 11.6 bitcast_dynamic-update-slice_fusion.11
  538.6 10.3 bitcast_dynamic-update-slice_fusion.12
  552.5 450.2 %while.56 = (s32[]{:T(128)}, f32[768]{0:T(1024)}, f32[768]{0:T(1024)}, f32[768,2304]{1,0:T(8,128)}, f32[768,768]{1,0:T(8,128)}, /*index=5*/f32[768]{0:T(1024)}, ...) while((s32[]{:T(128)}, f32[768]{0:T(1024)}, ...), condition=%wide.region_32.34_spmd.clone, body=%wide.region_15.33_spmd.clone.sunk | while | flops 35389038592 | bytes 976789248 | solution.py:353
  575.0 5.5 constant_dynamic-slice_fusion.7
  580.5 6.7 copy.145
  592.9 19.4 %fusion.418 = bf16[1024,3072]{1,0:T(8,128)(2,1)} fusion(f32[2,1024,3072]{2,1,0:T(8,128)} %get-tuple-element.1594, s32[]{:T(128)S(6)} %sub.736, bf16[3072,768]{1,0:T(8,128)(2,1)} %get-tuple-element.1593, pred[1024]{0:T(1024)(128)(4,1)S(1)} %copy-done.73, bf16[2,1024,768]{2,1,0:T(8,128)(2,1)} %get-tuple-element.1591), kind=kOutput, calls=%fused_computation.129.clone.1 | convolution fusion | flops 4910481408 | bytes 25167872 | tf_op jit(solution)/shard_map/while/body/eval_jaxpr/dot_general | solution.py:42
  612.3 10.1 multiply_reduce_fusion.17
  634.3 7.6 select_add_fusion.18
  643.0 5.9 multiply_reduce_fusion.18
  648.9 7.3 multiply_convert_fusion.13
  666.3 13.4 select_add_fusion.19
  687.6 6.4 fusion.427
  694.0 6.4 fusion.429
  702.0 6.4 fusion.436
  708.4 18.3 %multiply_reduce_fusion.19 = (f32[6,512]{1,0:T(8,128)S(1)}, f32[6,512]{1,0:T(8,128)S(1)}, f32[6,512,1024]{2,1,0:T(8,128)}) fusion(f32[6,512,1024]{2,1,0:T(8,128)} %copy-done.12, f32[6,512]{1,0:T(8,128)S(1)} %copy-done.43, pred[512,1024]{1,0:T(8,128)(4,1)S(1)} %copy-done.19, f32[6,512,1024]{2,1,0:T(8,128)} %fusion.436, f32[6,512]{1,0:T(8,128)S(1)} %copy-done.45, ...), kind=kOutput, calls=%fused_computation.148.clone.1 | convolution fusion | flops 434104320 | bytes 52486144 | tf_op jit(solution)/shard_map/while/body/eval_jaxpr/qhd,khd->hqk/dot_general | solution.py:152
  726.7 17.5 %multiply_convert_fusion.14 = (bf16[6,512,1024]{2,1,0:T(8,128)(2,1)S(1)}, bf16[6,512,1024]{2,1,0:T(8,128)(2,1)S(1)}) fusion(f32[6,512,1024]{2,1,0:T(8,128)} %get-tuple-element.1444, f32[6,512,1024]{2,1,0:T(8,128)} %copy-done.12, f32[6,512]{1,0:T(8,128)S(1)} %get-tuple-element.1445, f32[6,512]{1,0:T(8,128)S(1)} %copy-done.43, ...), kind=kLoop, calls=%fused_computation.147.clone.1 | loop fusion | flops 37748736 | bytes 63488000 | tf_op jit(solution)/shard_map/while/body/eval_jaxpr/convert_element_type | solution.py:159
  756.3 7.0 fusion.442
  765.2 7.8 select_add_fusion.15
  790.2 5.5 constant_dynamic-slice_fusion.7
  795.7 6.7 copy.145
  808.1 19.5 %fusion.418 = bf16[1024,3072]{1,0:T(8,128)(2,1)} fusion(f32[2,1024,3072]{2,1,0:T(8,128)} %get-tuple-element.1594, s32[]{:T(128)S(6)} %sub.736, bf16[3072,768]{1,0:T(8,128)(2,1)} %get-tuple-element.1593, pred[1024]{0:T(1024)(128)(4,1)S(1)} %copy-done.73, bf16[2,1024,768]{2,1,0:T(8,128)(2,1)} %get-tuple-element.1591), kind=kOutput, calls=%fused_computation.129.clone.1 | convolution fusion | flops 4910481408 | bytes 25167872 | tf_op jit(solution)/shard_map/while/body/eval_jaxpr/dot_general | solution.py:42
  827.6 10.1 multiply_reduce_fusion.17
  846.8 4.6 select_add_fusion.16
  851.4 10.0 select_add_fusion.18
  862.5 5.9 multiply_reduce_fusion.18
  868.4 7.3 multiply_convert_fusion.13
  885.8 14.8 select_add_fusion.19
  908.4 6.4 fusion.427
  914.9 6.4 fusion.429
  922.8 6.4 fusion.436
  929.2 18.3 %multiply_reduce_fusion.19 = (f32[6,512]{1,0:T(8,128)S(1)}, f32[6,512]{1,0:T(8,128)S(1)}, f32[6,512,1024]{2,1,0:T(8,128)}) fusion(f32[6,512,1024]{2,1,0:T(8,128)} %copy-done.12, f32[6,512]{1,0:T(8,128)S(1)} %copy-done.43, pred[512,1024]{1,0:T(8,128)(4,1)S(1)} %copy-done.19, f32[6,512,1024]{2,1,0:T(8,128)} %fusion.436, f32[6,512]{1,0:T(8,128)S(1)} %copy-done.45, ...), kind=kOutput, calls=%fused_computation.148.clone.1 | convolution fusion | flops 434104320 | bytes 52486144 | tf_op jit(solution)/shard_map/while/body/eval_jaxpr/qhd,khd->hqk/dot_general | solution.py:152
  947.5 17.5 %multiply_convert_fusion.14 = (bf16[6,512,1024]{2,1,0:T(8,128)(2,1)S(1)}, bf16[6,512,1024]{2,1,0:T(8,128)(2,1)S(1)}) fusion(f32[6,512,1024]{2,1,0:T(8,128)} %get-tuple-element.1444, f32[6,512,1024]{2,1,0:T(8,128)} %copy-done.12, f32[6,512]{1,0:T(8,128)S(1)} %get-tuple-element.1445, f32[6,512]{1,0:T(8,128)S(1)} %copy-done.43, ...), kind=kLoop, calls=%fused_computation.147.clone.1 | loop fusion | flops 37748736 | bytes 63488000 | tf_op jit(solution)/shard_map/while/body/eval_jaxpr/convert_element_type | solution.py:159
  977.2 7.0 fusion.442
  986.1 7.8 select_add_fusion.15
  1006.0 4.9 copy.119
  1014.6 8.8 copy.110
  1023.4 68.9 %all-to-all-done.3 = bf16[2,1024,768]{2,0,1:T(2,128)(2,1)S(1)} async-done(((bf16[2,1024,768]{2,0,1:T(2,128)(2,1)}), bf16[2,1024,768]{2,0,1:T(2,128)(2,1)S(1)}, u32[]{:S(2)}, u32[]{:S(2)}) %all-to-all-start.3) | async-done | bytes 3145760 | tf_op jit(solution)/shard_map/all_to_all | solution.py:359
  1092.3 4.7 all-to-all-start.1
  1097.7 93.8 %all-reduce.10 = (f32[768]{0:T(1024)S(1)}, f32[768]{0:T(1024)S(1)}, f32[768]{0:T(1024)S(1)}, f32[768]{0:T(1024)S(1)}) all-reduce(f32[768]{0:T(1024)S(1)} %copy-done.71, f32[768]{0:T(1024)S(1)} %copy-done.68, f32[768]{0:T(1024)S(1)} %copy-done.65, f32[768]{0:T(1024)S(1)} %get-tuple-element.640), channel_id=2, replica_groups=mesh['dp'=8,'fsdp'=4] {'dp','fsdp'}, use_global_device_ids=true, to_apply=%region_33.35.clone | all-reduce | flops 3072 | bytes 24576
  1201.2 4.5 gather_fusion.1
  1205.7 6.3 broadcast_select_fusion
  1212.0 71.3 %reduce-scatter.5.cloned.1.call-done = f32[24,2304]{1,0:T(8,128)} async-done(((f32[768,2304]{1,0:T(8,128)}), f32[24,2304]{1,0:T(8,128)}) %reduce-scatter.5.cloned.1.call-update) | async-done | bytes 221200 | tf_op jit(solution)/shard_map/reduce_scatter | solution.py:356
  1283.3 141.8 %reduce-scatter.9.cloned.1.call-done = f32[24,3072]{1,0:T(8,128)} async-done(((f32[768,3072]{1,0:T(8,128)}), f32[24,3072]{1,0:T(8,128)}) %reduce-scatter.9.cloned.1.call-update) | async-done | bytes 294928 | tf_op jit(solution)/shard_map/reduce_scatter | solution.py:356
  1425.1 141.9 %reduce-scatter.11.cloned.1.call-done = f32[96,768]{1,0:T(8,128)} async-done(((f32[3072,768]{1,0:T(8,128)}), f32[96,768]{1,0:T(8,128)}) %reduce-scatter.11.cloned.1.call-update) | async-done | bytes 294928 | tf_op jit(solution)/shard_map/reduce_scatter | solution.py:356
  (635 shorter events, 252.9 us)
Async XLA Ops:
  7.2 214.6 %all-gather.7.cloned.1.call-start = ((), (), s32[]{:S(2)}) async-start(), calls=%async_computation.9 | async-start | bytes 1216512 | tf_op jit(solution)/shard_map/all_gather | solution.py:321
  7.9 213.9 %all-gather.5.cloned.1.call-start = ((), (), s32[]{:S(2)}) async-start(), calls=%async_computation.8 | async-start | bytes 3649536 | tf_op jit(solution)/shard_map/all_gather | solution.py:320
  8.7 255.9 %all-gather.9.cloned.1.call-start = ((), (), s32[]{:S(2)}) async-start(), calls=%async_computation.10 | async-start | bytes 4866048 | tf_op jit(solution)/shard_map/all_gather | solution.py:324
  23.3 81.9 %all-to-all-start.2 = ((bf16[4,2,256,768]{3,2,1,0:T(8,128)(2,1)}), bf16[4,2,256,768]{3,2,1,0:T(8,128)(2,1)S(1)}, u32[]{:S(2)}, u32[]{:S(2)}) async-start(bf16[4,2,256,768]{3,2,1,0:T(8,128)(2,1)} %pad_maximum_fusion.3), calls=%async_computation.2 | async-start | bytes 6291456 | tf_op jit(solution)/shard_map/all_to_all | solution.py:307
  29.6 299.5 %all-gather.11.cloned.1.call-start = ((), (), s32[]{:S(2)}) async-start(), calls=%async_computation.11 | async-start | bytes 4866048 | tf_op jit(solution)/shard_map/all_gather | solution.py:325
  105.2 112.0 %copy-start.91 = (s32[1,8]{1,0:T(1,128)S(1)}, s32[1,8]{1,0:T(1,128)}, u32[]{:S(2)}) copy-start(s32[1,8]{1,0:T(1,128)} %param.20) | copy-start | bytes 100
  105.2 114.5 %all-to-all-start = ((bf16[8,256,768]{2,1,0:T(8,128)(2,1)}), bf16[8,256,768]{2,1,0:T(8,128)(2,1)}, u32[]{:S(2)}, u32[]{:S(2)}) async-start(bf16[8,256,768]{2,1,0:T(8,128)(2,1)} %get-tuple-element.1069), calls=%async_computation | async-start | bytes 6291456 | tf_op jit(solution)/shard_map/all_to_all | solution.py:305
  110.0 1102.0 %reduce-scatter.7.cloned.1.call-start = ((), (), s32[]{:S(2)}) async-start(), calls=%async_computation.13 | async-start | bytes 2433024 | tf_op jit(solution)/shard_map/reduce_scatter | solution.py:356
  419.3 7.7 slice-start.4
  427.0 11.4 copy-start.40
  427.0 11.4 copy-start.79
  438.5 12.0 copy-start.8
  438.5 12.0 copy-start.53
  438.5 12.0 copy-start.57
  438.5 12.0 copy-start.75
  438.5 12.0 copy-start.77
  519.3 7.6 slice-start.4
  526.9 11.6 copy-start.40
  526.9 11.6 copy-start.79
  538.6 12.0 copy-start.8
  538.6 12.0 copy-start.53
  538.6 12.0 copy-start.57
  538.6 12.0 copy-start.75
  538.6 12.0 copy-start.77
  561.0 11.1 copy-start.9
  574.5 12.6 copy-start.4
  590.8 72.1 %copy-start.15 = (bf16[1024,12,64]{0,2,1:T(8,128)(2,1)}, bf16[1024,12,64]{0,2,1:T(8,128)(2,1)S(1)}, u32[]{:S(2)}) copy-start(bf16[1024,12,64]{0,2,1:T(8,128)(2,1)S(1)} %get-tuple-element.1432) | copy-start | bytes 4718596 | tf_op jit(solution)/shard_map/while
  612.3 10.1 copy-start.5
  612.3 10.1 copy-start.24
  626.6 7.7 slice-start.8
  634.3 7.6 copy-start.17
  656.3 8.0 slice-start
  751.9 13.3 slice-start.6
  756.3 8.9 slice-start.7
  765.2 7.9 copy-start.36
  765.2 10.8 copy-start.49
  765.2 10.8 copy-start.55
  765.2 10.8 copy-start.59
  765.2 10.7 copy-start.62
  776.2 11.1 copy-start.9
  789.7 12.6 copy-start.4
  806.0 76.4 %copy-start.15 = (bf16[1024,12,64]{0,2,1:T(8,128)(2,1)}, bf16[1024,12,64]{0,2,1:T(8,128)(2,1)S(1)}, u32[]{:S(2)}) copy-start(bf16[1024,12,64]{0,2,1:T(8,128)(2,1)S(1)} %get-tuple-element.1432) | copy-start | bytes 4718596 | tf_op jit(solution)/shard_map/while
  827.6 10.1 copy-start.5
  827.6 10.1 copy-start.24
  841.8 9.6 slice-start.8
  851.4 10.1 copy-start.17
  875.8 8.0 slice-start
  972.8 13.3 slice-start.6
  977.1 8.9 slice-start.7
  986.0 7.9 copy-start.36
  986.1 10.8 copy-start.49
  986.1 10.8 copy-start.55
  986.1 10.8 copy-start.59
  986.1 10.7 copy-start.62
  1002.7 280.6 %reduce-scatter.5.cloned.1.call-start = ((), (), s32[]{:S(2)}) async-start(), calls=%async_computation.12 | async-start | bytes 7299072 | tf_op jit(solution)/shard_map/reduce_scatter | solution.py:356
  1003.3 421.8 %reduce-scatter.9.cloned.1.call-start = ((), (), s32[]{:S(2)}) async-start(), calls=%async_computation.14 | async-start | bytes 9732096 | tf_op jit(solution)/shard_map/reduce_scatter | solution.py:356
  1004.0 563.0 %reduce-scatter.11.cloned.1.call-start = ((), (), s32[]{:S(2)}) async-start(), calls=%async_computation.15 | async-start | bytes 9732096 | tf_op jit(solution)/shard_map/reduce_scatter | solution.py:356
  1010.9 81.4 %all-to-all-start.3 = ((bf16[2,1024,768]{2,0,1:T(2,128)(2,1)}), bf16[2,1024,768]{2,0,1:T(2,128)(2,1)S(1)}, u32[]{:S(2)}, u32[]{:S(2)}) async-start(bf16[2,1024,768]{2,0,1:T(2,128)(2,1)} %copy.119), calls=%async_computation.3 | async-start | bytes 6291456 | tf_op jit(solution)/shard_map/all_to_all | solution.py:359
  1023.4 73.6 %copy-start.93 = (s32[1,8]{1,0:T(1,128)S(1)}, s32[1,8]{1,0:T(1,128)}, u32[]{:S(2)}) copy-start(s32[1,8]{1,0:T(1,128)} %param.21) | copy-start | bytes 100
  1023.4 74.3 %copy-start.65 = (f32[768]{0:T(1024)S(1)}, f32[768]{0:T(1024)}, u32[]{:S(2)}) copy-start(f32[768]{0:T(1024)} %get-tuple-element.639) | copy-start | bytes 9220
  1023.4 74.3 %copy-start.68 = (f32[768]{0:T(1024)S(1)}, f32[768]{0:T(1024)}, u32[]{:S(2)}) copy-start(f32[768]{0:T(1024)} %get-tuple-element.636) | copy-start | bytes 9220
  1023.4 74.3 %copy-start.71 = (f32[768]{0:T(1024)S(1)}, f32[768]{0:T(1024)}, u32[]{:S(2)}) copy-start(f32[768]{0:T(1024)} %get-tuple-element.635) | copy-start | bytes 9220
  1092.3 102.2 %all-to-all-start.1 = ((bf16[2,1024,768]{2,0,1:T(2,128)(2,1)}), bf16[2,1024,768]{2,0,1:T(2,128)(2,1)}, u32[]{:S(2)}, u32[]{:S(2)}) async-start(bf16[2,1024,768]{2,0,1:T(2,128)(2,1)} %copy.110), calls=%async_computation.1 | async-start | bytes 6291456 | tf_op jit(solution)/shard_map/all_to_all | solution.py:358
  1205.7 361.3 %copy-start.1 = (bf16[8,256,768]{2,1,0:T(8,128)(2,1)S(1)}, bf16[8,256,768]{2,1,0:T(8,128)(2,1)}, u32[]{:S(2)}) copy-start(bf16[8,256,768]{2,1,0:T(8,128)(2,1)} %param.19) | copy-start | bytes 9437188
  (141 other events, 490.9 us)
Sparse Core Ops, SparseCore 0:
  10.8 96.0 all-gather.6
  109.7 88.6 all-gather.4
  201.2 63.2 all-gather.8
  267.2 61.8 all-gather.10
  1002.8 153.7 reduce-scatter.6
  1162.8 120.4 reduce-scatter.4
  1289.8 135.2 reduce-scatter.8
  1431.6 135.3 reduce-scatter.10
